TPU v7x, 32 devices: a whole 2x2x4 slice. The times are simulated.
32 devices in a mesh: dp: 16 (over z, x, core), tensor: 2 (over y).
Axes of the slice: x: 2, y: 2, z: 4, core: 2. Of those that a mesh axis runs over, the one named last changes fastest.
Arguments:
- tokens: bfloat16 [16, 736, 1152], P('dp', 'tensor'), may hold values from -6 to 6
- cotangent: bfloat16 [16, 736, 1152], P('dp', 'tensor'), may hold values from -6 to 6
- counts: int32 [16], P('dp'), may hold values from 638 to 729
- joint_weight: float32 [1152, 3, 1152], P('dp', None, 'tensor'), may hold values from -0.1875 to 0.1875
- joint_moment: float32 [1152, 3, 1152], P('dp', None, 'tensor'), may hold values from -0.0014648438 to 0.0014648438
- joint_square: float32 [1152, 3, 1152], P('dp', None, 'tensor'), may hold values from 4.53793e-09 to 3.630344e-08
- output_weight: float32 [1152, 1152], P('tensor', 'dp'), may hold values from -0.5 to 0.5
- output_moment: float32 [1152, 1152], P('tensor', 'dp'), may hold values from -0.0029296875 to 0.0029296875
- output_square: float32 [1152, 1152], P('tensor', 'dp'), may hold values from 1.815172e-08 to 1.4521376e-07
- expand_weight: float32 [1152, 4304], P('dp', 'tensor'), may hold values from -0.1875 to 0.1875
- expand_moment: float32 [1152, 4304], P('dp', 'tensor'), may hold values from -0.0029296875 to 0.0029296875
- expand_square: float32 [1152, 4304], P('dp', 'tensor'), may hold values from 1.815172e-08 to 1.4521376e-07
- reduce_weight: float32 [4304, 1152], P('tensor', 'dp'), may hold values from -0.09375 to 0.09375
- reduce_moment: float32 [4304, 1152], P('tensor', 'dp'), may hold values from -0.005859375 to 0.005859375
- reduce_square: float32 [4304, 1152], P('tensor', 'dp'), may hold values from 7.260688e-08 to 5.8085504e-07
- norm_gains: float32 [2, 1152], replicated, may hold values from 0.5 to 1.5
- gains_moment: float32 [2, 1152], replicated, may hold values from -0.009765625 to 0.009765625
- gains_square: float32 [2, 1152], replicated, may hold values from 2.0168576e-07 to 1.6134861e-06
- shifts: float32 [4, 1152], replicated, may hold values from -3 to 3
- shifts_moment: float32 [4, 1152], replicated, may hold values from -0.009765625 to 0.009765625
- shifts_square: float32 [4, 1152], replicated, may hold values from 2.0168576e-07 to 1.6134861e-06
- head_bias: float32 [2, 1152], P(None, 'tensor'), may hold values from -3 to 3
- head_moment: float32 [2, 1152], P(None, 'tensor'), may hold values from -0.0029296875 to 0.0029296875
- head_square: float32 [2, 1152], P(None, 'tensor'), may hold values from 1.815172e-08 to 1.4521376e-07
- hidden_bias: float32 [4304], P('tensor'), may hold values from -3 to 3
- hidden_moment: float32 [4304], P('tensor'), may hold values from -0.0029296875 to 0.0029296875
- hidden_square: float32 [4304], P('tensor'), may hold values from 1.815172e-08 to 1.4521376e-07
Outputs:
- layer_out: bfloat16 [16, 736, 1152], P('dp', 'tensor')
- input_grad: bfloat16 [16, 736, 1152], P('dp', 'tensor')
- grad_norm: float32 [], replicated
- joint_new: float32 [1152, 3, 1152], P('dp', None, 'tensor')
- joint_moment_new: float32 [1152, 3, 1152], P('dp', None, 'tensor')
- joint_square_new: float32 [1152, 3, 1152], P('dp', None, 'tensor')
- joint_copy: bfloat16 [1152, 3, 1152], P('dp', None, 'tensor')
- output_new: float32 [1152, 1152], P('tensor', 'dp')
- output_moment_new: float32 [1152, 1152], P('tensor', 'dp')
- output_square_new: float32 [1152, 1152], P('tensor', 'dp')
- output_copy: bfloat16 [1152, 1152], P('tensor', 'dp')
- expand_new: float32 [1152, 4304], P('dp', 'tensor')
- expand_moment_new: float32 [1152, 4304], P('dp', 'tensor')
- expand_square_new: float32 [1152, 4304], P('dp', 'tensor')
- expand_copy: bfloat16 [1152, 4304], P('dp', 'tensor')
- reduce_new: float32 [4304, 1152], P('tensor', 'dp')
- reduce_moment_new: float32 [4304, 1152], P('tensor', 'dp')
- reduce_square_new: float32 [4304, 1152], P('tensor', 'dp')
- reduce_copy: bfloat16 [4304, 1152], P('tensor', 'dp')
- gains_new: float32 [2, 1152], replicated
- gains_moment_new: float32 [2, 1152], replicated
- gains_square_new: float32 [2, 1152], replicated
- shifts_new: float32 [4, 1152], replicated
- shifts_moment_new: float32 [4, 1152], replicated
- shifts_square_new: float32 [4, 1152], replicated
- head_new: float32 [2, 1152], P(None, 'tensor')
- head_moment_new: float32 [2, 1152], P(None, 'tensor')
- head_square_new: float32 [2, 1152], P(None, 'tensor')
- hidden_new: float32 [4304], P('tensor')
- hidden_moment_new: float32 [4304], P('tensor')
- hidden_square_new: float32 [4304], P('tensor')
Inputs may be any that keep to these rules, and one draw needn't show every extreme that they name: `counts`: valid tokens of each image; key slots from there up to 736 are padding.
All inputs are finite; a program needn't handle non-finite values.
Results may differ from a plain program's by a relative error of at most 0.01.
Values may be sent and summed in bfloat16 or wider, within the bound.
A program may use at most 192 MiB of HBM per device.

v0:
```python
import jax
import jax.numpy as jnp
from jax import lax
from jax.sharding import PartitionSpec as P

HD = 72
STEP = 4
norm_eps = 1e-06
clip_limit = 1.0
matrix_rate = 0.03
vector_rate = 0.3
decay_rate = 0.1
adam_eps = 1e-08
mask_fill = -1e30


def layer_norm(values, gain, shift):
    center = jnp.mean(values, axis=-1, keepdims=True)
    centred = values - center
    spread = jnp.mean(centred * centred, axis=-1, keepdims=True)
    return centred * lax.rsqrt(spread + norm_eps) * gain + shift


def gelu_tanh(values):
    return jax.nn.gelu(values, approximate=True)


def whole_rows(part):
    return lax.all_gather(part, "tensor", axis=1, tiled=True)


def share_rows(full):
    return lax.psum_scatter(
        full.astype(jnp.bfloat16), "tensor", scatter_dimension=1, tiled=True
    ).astype(jnp.float32)


def scatter_sum(part, dim):
    return lax.psum_scatter(
        part.astype(jnp.bfloat16), "dp", scatter_dimension=dim, tiled=True
    ).astype(jnp.float32)


def split_heads(joint):
    length = joint.shape[0]
    heads_local = joint.shape[2] // HD
    query = joint[:, 0].reshape(length, heads_local, HD)
    keys = joint[:, 1].reshape(length, heads_local, HD)
    values = joint[:, 2].reshape(length, heads_local, HD)
    return (query, keys, values)


def masked_scores(query, keys, count):
    length = query.shape[0]
    scores = jnp.einsum("qhd,khd->hqk", query, keys, preferred_element_type=jnp.float32) * HD ** (
        -0.5
    )
    valid = jnp.arange(length, dtype=jnp.int32) < count
    return jnp.where(valid[None, None, :], scores, mask_fill)


def attend(joint, count):
    query, keys, values = split_heads(joint)
    scores = masked_scores(query, keys, count)
    top = jnp.max(scores, axis=-1, keepdims=True)
    total = jnp.sum(jnp.exp(scores - top), axis=-1, keepdims=True)
    logsum = top + jnp.log(total)
    probs = jnp.exp(scores - logsum)
    mixed = jnp.einsum(
        "hqk,khd->qhd", probs.astype(jnp.bfloat16), values, preferred_element_type=jnp.float32
    )
    return (mixed.reshape(joint.shape[0], joint.shape[2]).astype(jnp.bfloat16), logsum[:, :, 0])


def attend_back(joint, mixed_grad, logsum, count):
    query, keys, values = split_heads(joint)
    length = joint.shape[0]
    grad_heads = mixed_grad.reshape(length, joint.shape[2] // HD, HD)
    scores = masked_scores(query, keys, count)
    probs = jnp.exp(scores - logsum[:, :, None])
    value_grad = jnp.einsum(
        "hqk,qhd->khd", probs.astype(jnp.bfloat16), grad_heads, preferred_element_type=jnp.float32
    )
    prob_grad = jnp.einsum("qhd,khd->hqk", grad_heads, values, preferred_element_type=jnp.float32)
    inner = jnp.sum(probs * prob_grad, axis=-1, keepdims=True)
    score_grad = (probs * (prob_grad - inner)).astype(jnp.bfloat16)
    query_grad = jnp.einsum(
        "hqk,khd->qhd", score_grad, keys, preferred_element_type=jnp.float32
    ) * HD ** (-0.5)
    key_grad = jnp.einsum(
        "hqk,qhd->khd", score_grad, query, preferred_element_type=jnp.float32
    ) * HD ** (-0.5)
    stacked = jnp.stack([query_grad, key_grad, value_grad], axis=1)
    return stacked.reshape(length, 3, joint.shape[2]).astype(jnp.bfloat16)


def forward_pass(tokens, counts, weights, small):
    joint_w, expand_w, output_w, reduce_w = weights
    norm_gains, shifts, head_bias, hidden_bias = small
    rows = tokens.astype(jnp.float32)
    normed, first_back = jax.vjp(layer_norm, rows, norm_gains[0], shifts[0])
    normed_whole = whole_rows(normed.astype(jnp.bfloat16))
    joint = jnp.einsum("bsd,dch->bsch", normed_whole, joint_w, preferred_element_type=jnp.float32)
    bias = jnp.stack([head_bias[0], jnp.zeros_like(head_bias[0]), head_bias[1]])
    joint = (joint + bias).astype(jnp.bfloat16)
    mixed, logsum = lax.map(lambda pair: attend(pair[0], pair[1]), (joint, counts))
    branch = (
        share_rows(jnp.einsum("bsh,hd->bsd", mixed, output_w, preferred_element_type=jnp.float32))
        + shifts[2]
    )
    middle = rows + branch
    second, second_back = jax.vjp(layer_norm, middle, norm_gains[1], shifts[1])
    second_whole = whole_rows(second.astype(jnp.bfloat16))
    before = (
        jnp.einsum("bsd,df->bsf", second_whole, expand_w, preferred_element_type=jnp.float32)
        + hidden_bias
    )
    active, gelu_back = jax.vjp(gelu_tanh, before)
    active = active.astype(jnp.bfloat16)
    result = (
        share_rows(jnp.einsum("bsf,fd->bsd", active, reduce_w, preferred_element_type=jnp.float32))
        + shifts[3]
    )
    saved = (
        first_back,
        normed_whole,
        joint,
        mixed,
        logsum,
        second_back,
        second_whole,
        active,
        gelu_back,
    )
    return (middle + result, saved)


def adamw_step(weight, grad, moment, square, factor, rate, decay):
    clipped = grad * factor
    moment_new = 0.5 * moment + 0.5 * clipped
    square_new = 0.5 * square + 0.5 * clipped * clipped
    correct = 1.0 - 0.5**STEP
    update = moment_new / correct / (jnp.sqrt(square_new / correct) + adam_eps)
    return (weight - rate * (update + decay * weight), moment_new, square_new)


def squares(values):
    return jnp.sum(values * values)


def on_device(
    tokens,
    cotangent,
    counts,
    joint_weight,
    joint_moment,
    joint_square,
    output_weight,
    output_moment,
    output_square,
    expand_weight,
    expand_moment,
    expand_square,
    reduce_weight,
    reduce_moment,
    reduce_square,
    norm_gains,
    gains_moment,
    gains_square,
    shifts,
    shifts_moment,
    shifts_square,
    head_bias,
    head_moment,
    head_square,
    hidden_bias,
    hidden_moment,
    hidden_square,
):
    first_pair = (
        lax.all_gather(joint_weight.astype(jnp.bfloat16), "dp", axis=0, tiled=True),
        lax.all_gather(expand_weight.astype(jnp.bfloat16), "dp", axis=0, tiled=True),
    )
    second_pair = (
        lax.all_gather(output_weight.astype(jnp.bfloat16), "dp", axis=1, tiled=True),
        lax.all_gather(reduce_weight.astype(jnp.bfloat16), "dp", axis=1, tiled=True),
    )
    weights = (first_pair[0], first_pair[1], second_pair[0], second_pair[1])
    small = (norm_gains, shifts, head_bias, hidden_bias)
    layer_rows, saved = forward_pass(tokens, counts, weights, small)
    layer_out = layer_rows.astype(jnp.bfloat16)
    first_back, normed_whole, joint, mixed, logsum, second_back, second_whole, active, gelu_back = (
        saved
    )
    joint_w, expand_w, output_w, reduce_w = weights
    grad_rows = cotangent.astype(jnp.float32)
    grad_whole = whole_rows(cotangent)
    reduce_grad = jnp.einsum("bsf,bsd->fd", active, grad_whole, preferred_element_type=jnp.float32)
    active_grad = jnp.einsum(
        "bsd,fd->bsf", grad_whole, reduce_w, preferred_element_type=jnp.float32
    )
    before_grad = gelu_back(active_grad)[0].astype(jnp.bfloat16)
    expand_grad = jnp.einsum(
        "bsd,bsf->df", second_whole, before_grad, preferred_element_type=jnp.float32
    )
    hidden_grad = jnp.sum(before_grad, axis=(0, 1), dtype=jnp.float32)
    second_grad = share_rows(
        jnp.einsum("bsf,df->bsd", before_grad, expand_w, preferred_element_type=jnp.float32)
    )
    middle_part, gain_two, shift_two = second_back(second_grad)
    middle_grad = grad_rows + middle_part
    branch_grad = middle_grad.astype(jnp.bfloat16)
    branch_whole = whole_rows(branch_grad)
    output_grad = jnp.einsum("bsh,bsd->hd", mixed, branch_whole, preferred_element_type=jnp.float32)
    mixed_grad = jnp.einsum(
        "bsd,hd->bsh", branch_whole, output_w, preferred_element_type=jnp.float32
    ).astype(jnp.bfloat16)
    joint_grad = lax.map(
        lambda group: attend_back(group[0], group[1], group[2], group[3]),
        (joint, mixed_grad, logsum, counts),
    )
    joint_weight_grad = jnp.einsum(
        "bsd,bsch->dch", normed_whole, joint_grad, preferred_element_type=jnp.float32
    )
    head_grad = jnp.sum(joint_grad[:, :, 0::2], axis=(0, 1), dtype=jnp.float32)
    first_grad = share_rows(
        jnp.einsum("bsch,dch->bsd", joint_grad, joint_w, preferred_element_type=jnp.float32)
    )
    rows_part, gain_one, shift_one = first_back(first_grad)
    input_grad = (middle_grad + rows_part).astype(jnp.bfloat16)
    gain_grad = jnp.stack([gain_one, gain_two])
    shift_grad = jnp.stack(
        [
            shift_one,
            shift_two,
            jnp.sum(branch_grad, axis=(0, 1), dtype=jnp.float32),
            jnp.sum(grad_rows, axis=(0, 1)),
        ]
    )
    joint_sum, expand_sum = (scatter_sum(joint_weight_grad, 0), scatter_sum(expand_grad, 0))
    output_sum, reduce_sum = (scatter_sum(output_grad, 1), scatter_sum(reduce_grad, 1))
    gain_sum, shift_sum = lax.psum((gain_grad, shift_grad), ("dp", "tensor"))
    head_sum, hidden_sum = lax.psum((head_grad, hidden_grad), "dp")
    data_count = lax.axis_size("dp")
    split_count = lax.axis_size("tensor")
    owned = squares(joint_sum) + squares(expand_sum) + squares(output_sum) + squares(reduce_sum)
    shared = (squares(head_sum) + squares(hidden_sum)) / data_count
    everywhere = (squares(gain_sum) + squares(shift_sum)) / (data_count * split_count)
    grad_norm = jnp.sqrt(lax.psum(owned + shared + everywhere, ("dp", "tensor")))
    factor = clip_limit / jnp.maximum(grad_norm, clip_limit)
    joint_state = adamw_step(
        joint_weight, joint_sum, joint_moment, joint_square, factor, matrix_rate, decay_rate
    )
    output_state = adamw_step(
        output_weight, output_sum, output_moment, output_square, factor, matrix_rate, decay_rate
    )
    expand_state = adamw_step(
        expand_weight, expand_sum, expand_moment, expand_square, factor, matrix_rate, decay_rate
    )
    reduce_state = adamw_step(
        reduce_weight, reduce_sum, reduce_moment, reduce_square, factor, matrix_rate, decay_rate
    )
    gains_state = adamw_step(
        norm_gains, gain_sum, gains_moment, gains_square, factor, vector_rate, 0.0
    )
    shifts_state = adamw_step(
        shifts, shift_sum, shifts_moment, shifts_square, factor, vector_rate, 0.0
    )
    head_state = adamw_step(head_bias, head_sum, head_moment, head_square, factor, vector_rate, 0.0)
    hidden_state = adamw_step(
        hidden_bias, hidden_sum, hidden_moment, hidden_square, factor, vector_rate, 0.0
    )
    return (
        layer_out,
        input_grad,
        grad_norm,
        joint_state[0],
        joint_state[1],
        joint_state[2],
        joint_state[0].astype(jnp.bfloat16),
        output_state[0],
        output_state[1],
        output_state[2],
        output_state[0].astype(jnp.bfloat16),
        expand_state[0],
        expand_state[1],
        expand_state[2],
        expand_state[0].astype(jnp.bfloat16),
        reduce_state[0],
        reduce_state[1],
        reduce_state[2],
        reduce_state[0].astype(jnp.bfloat16),
        gains_state[0],
        gains_state[1],
        gains_state[2],
        shifts_state[0],
        shifts_state[1],
        shifts_state[2],
        head_state[0],
        head_state[1],
        head_state[2],
        hidden_state[0],
        hidden_state[1],
        hidden_state[2],
    )


def solution(mesh):
    in_specs = (
        P("dp", "tensor", None),
        P("dp", "tensor", None),
        P("dp"),
        P("dp", None, "tensor"),
        P("dp", None, "tensor"),
        P("dp", None, "tensor"),
        P("tensor", "dp"),
        P("tensor", "dp"),
        P("tensor", "dp"),
        P("dp", "tensor"),
        P("dp", "tensor"),
        P("dp", "tensor"),
        P("tensor", "dp"),
        P("tensor", "dp"),
        P("tensor", "dp"),
        P(),
        P(),
        P(),
        P(),
        P(),
        P(),
        P(None, "tensor"),
        P(None, "tensor"),
        P(None, "tensor"),
        P("tensor"),
        P("tensor"),
        P("tensor"),
    )
    out_specs = (
        P("dp", "tensor", None),
        P("dp", "tensor", None),
        P(),
        P("dp", None, "tensor"),
        P("dp", None, "tensor"),
        P("dp", None, "tensor"),
        P("dp", None, "tensor"),
        P("tensor", "dp"),
        P("tensor", "dp"),
        P("tensor", "dp"),
        P("tensor", "dp"),
        P("dp", "tensor"),
        P("dp", "tensor"),
        P("dp", "tensor"),
        P("dp", "tensor"),
        P("tensor", "dp"),
        P("tensor", "dp"),
        P("tensor", "dp"),
        P("tensor", "dp"),
        P(),
        P(),
        P(),
        P(),
        P(),
        P(),
        P(None, "tensor"),
        P(None, "tensor"),
        P(None, "tensor"),
        P("tensor"),
        P("tensor"),
        P("tensor"),
    )
    return jax.shard_map(
        on_device, mesh=mesh, in_specs=in_specs, out_specs=out_specs, check_vma=False
    )
```

profile of v0, /device:TPU:0, one launch (start us, length us, event | category | flops | bytes accessed | tf_op | source)
XLA Modules:
  0.0 853.5 jit_solution(2574007469518018370)
XLA Ops:
  12.6 2.4 fusion.23
  17.5 29.0 %all-gather.9.cloned.1.call-done = bf16[1,736,1152]{2,1,0:T(8,128)(2,1)} async-done(((bf16[1,368,1152]{2,1,0:T(8,128)(2,1)}), bf16[1,736,1152]{2,1,0:T(8,128)(2,1)}) %all-gather.9.cloned.1.call-update) | async-done | bytes 1695760 | tf_op jit(solution)/shard_map/all_gather | solution.py:29
  46.5 54.5 %all-gather.11.cloned.1.call-done = bf16[1152,3,576]{2,0,1:T(8,128)(2,1)} async-done(((bf16[72,3,576]{2,0,1:T(8,128)(2,1)}), bf16[1152,3,576]{2,0,1:T(8,128)(2,1)}) %all-gather.11.cloned.1.call-update) | async-done | bytes 3981328 | tf_op jit(solution)/shard_map/all_gather | solution.py:181
  101.0 6.4 add_convert_fusion
  107.7 8.6 %fusion = (f32[8,736]{1,0:T(8,128)S(1)}, f32[8,736,736]{1,2,0:T(8,128)}) fusion(pred[736]{0:T(1024)(128)(4,1)S(1)} %iota_compare_fusion, bf16[736,8,72]{0,2,1:T(8,128)(2,1)S(1)} %bitcast.96, bf16[736,8,72]{0,2,1:T(8,128)(2,1)S(1)} %bitcast.94), kind=kOutput, calls=%fused_computation.5 | convolution fusion | flops 637028608 | bytes 19054304 | tf_op jit(solution)/shard_map/while/body/eval_jaxpr/qhd,khd->hqk/dot_general | solution.py:55
  116.3 10.0 %exponential_reduce_fusion = f32[8,736]{1,0:T(8,128)S(1)} fusion(f32[8,736,736]{1,2,0:T(8,128)} %get-tuple-element.122, f32[8,736]{1,0:T(8,128)S(1)} %get-tuple-element.121, pred[736]{0:T(1024)(128)(4,1)S(1)} %iota_compare_fusion), kind=kLoop, calls=%fused_computation.3 | loop fusion | flops 17328384 | bytes 17382112 | tf_op jit(solution)/shard_map/while/body/eval_jaxpr/reduce_sum | solution.py:66
  126.3 8.2 fusion.1
  134.6 3.5 copy-done.1
  139.8 1.8 all-gather.13.cloned.1.call-done
  141.6 4.3 fusion.10
  146.9 25.5 %reduce-scatter.17.cloned.1.call-done = bf16[1,368,1152]{2,1,0:T(8,128)(2,1)} async-done(((bf16[1,736,1152]{2,1,0:T(8,128)(2,1)}), bf16[1,368,1152]{2,1,0:T(8,128)(2,1)}) %reduce-scatter.17.cloned.1.call-update) | async-done | bytes 847888 | tf_op jit(solution)/shard_map/reduce_scatter | solution.py:33
  179.3 50.8 %all-gather.17.cloned.1.call-done = bf16[1152,2152]{1,0:T(8,128)(2,1)} async-done(((bf16[72,2152]{1,0:T(8,128)(2,1)}), bf16[1152,2152]{1,0:T(8,128)(2,1)}) %all-gather.17.cloned.1.call-update) | async-done | bytes 4958224 | tf_op jit(solution)/shard_map/all_gather | solution.py:182
  230.1 29.2 %all-gather.15.cloned.1.call-done = bf16[1,736,1152]{2,1,0:T(8,128)(2,1)} async-done(((bf16[1,368,1152]{2,1,0:T(8,128)(2,1)}), bf16[1,736,1152]{2,1,0:T(8,128)(2,1)}) %all-gather.15.cloned.1.call-update) | async-done | bytes 1695760 | tf_op jit(solution)/shard_map/all_gather | solution.py:29
  259.4 10.1 %fusion.38 = f32[736,2152]{1,0:T(8,128)} fusion(bf16[1152,2152]{1,0:T(8,128)(2,1)} %all-gather.17.cloned.1.call-done, bf16[1,736,1152]{2,1,0:T(8,128)(2,1)} %all-gather.15.cloned.1.call-done), kind=kOutput, calls=%fused_computation.72 | convolution fusion | flops 3649241088 | bytes 12989440 | tf_op jit(solution)/shard_map/bsd,df->bsf/dot_general | solution.py:115
  269.5 20.1 %all-gather.21.cloned.1.call-done = bf16[1,736,1152]{2,1,0:T(8,128)(2,1)} async-done(((bf16[1,368,1152]{2,1,0:T(8,128)(2,1)}), bf16[1,736,1152]{2,1,0:T(8,128)(2,1)}) %all-gather.21.cloned.1.call-update) | async-done | bytes 1695760 | tf_op jit(solution)/shard_map/all_gather | solution.py:29
  289.6 57.9 %all-gather.19.cloned.1.call-done = bf16[2152,1152]{0,1:T(8,128)(2,1)} async-done(((bf16[2152,72]{0,1:T(8,128)(2,1)}), bf16[2152,1152]{0,1:T(8,128)(2,1)}) %all-gather.19.cloned.1.call-update) | async-done | bytes 4958224 | tf_op jit(solution)/shard_map/all_gather | solution.py:186
  347.5 11.3 %convert_reduce_fusion = (f32[2152]{0:T(1024)S(1)}, bf16[736,2152]{1,0:T(8,128)(2,1)S(1)}) fusion(f32[736,2152]{1,0:T(8,128)} %fusion.38, f32[2152]{0:T(1024)S(1)} %copy-done.46, bf16[2152,1152]{0,1:T(8,128)(2,1)} %all-gather.19.cloned.1.call-done, bf16[1,736,1152]{2,1,0:T(8,128)(2,1)} %all-gather.21.cloned.1.call-done), kind=kOutput, calls=%fused_computation.18 | convolution fusion | flops 3685668096 | bytes 16174400 | tf_op jit(solution)/shard_map/bsd,fd->bsf/dot_general | solution.py:199
  360.5 8.2 fusion.13
  368.9 11.1 %fusion.12 = bf16[1,736,1152]{2,1,0:T(8,128)(2,1)} fusion(bf16[2152,1152]{0,1:T(8,128)(2,1)} %all-gather.19.cloned.1.call-done, f32[736,2152]{1,0:T(8,128)} %fusion.38, f32[2152]{0:T(1024)S(1)} %copy-done.46), kind=kOutput, calls=%fused_computation.31 | convolution fusion | flops 3665927680 | bytes 12998048 | tf_op jit(solution)/shard_map/bsf,fd->bsd/dot_general | solution.py:121
  380.1 14.7 %reduce-scatter.21.cloned.1.call-done = bf16[1,368,1152]{2,1,0:T(8,128)(2,1)} async-done(((bf16[1,736,1152]{2,1,0:T(8,128)(2,1)}), bf16[1,368,1152]{2,1,0:T(8,128)(2,1)}) %reduce-scatter.21.cloned.1.call-update) | async-done | bytes 847888 | tf_op jit(solution)/shard_map/reduce_scatter | solution.py:33
  394.8 2.0 fusion.27
  396.8 27.5 %reduce-scatter.19.cloned.1.call-done = bf16[1,368,1152]{2,1,0:T(8,128)(2,1)} async-done(((bf16[1,736,1152]{2,1,0:T(8,128)(2,1)}), bf16[1,368,1152]{2,1,0:T(8,128)(2,1)}) %reduce-scatter.19.cloned.1.call-update) | async-done | bytes 847888 | tf_op jit(solution)/shard_map/reduce_scatter | solution.py:33
  424.4 3.3 fusion.78
  429.0 28.7 %all-gather.23.cloned.1.call-done = bf16[1,736,1152]{2,1,0:T(8,128)(2,1)} async-done(((bf16[1,368,1152]{2,1,0:T(8,128)(2,1)}), bf16[1,736,1152]{2,1,0:T(8,128)(2,1)}) %all-gather.23.cloned.1.call-update) | async-done | bytes 1695760 | tf_op jit(solution)/shard_map/all_gather | solution.py:29
  457.7 4.5 convolution_convert_fusion.6
  462.4 10.1 %convolution_convert_fusion = bf16[2152,1152]{0,1:T(8,128)(2,1)} fusion(bf16[1,736,1152]{2,1,0:T(8,128)(2,1)} %all-gather.21.cloned.1.call-done, f32[736,2152]{1,0:T(8,128)} %fusion.38, f32[2152]{0:T(1024)S(1)} %copy-done.46), kind=kOutput, calls=%fused_computation.6 | convolution fusion | flops 3667558912 | bytes 12998048 | tf_op jit(solution)/shard_map/bsf,bsd->fd/dot_general | solution.py:198
  472.6 9.1 %convolution_convert_fusion.1 = bf16[1152,2152]{1,0:T(8,128)(2,1)} fusion(bf16[736,2152]{1,0:T(8,128)(2,1)} %copy-done.47, bf16[1,736,1152]{2,1,0:T(8,128)(2,1)} %all-gather.15.cloned.1.call-done), kind=kOutput, calls=%fused_computation.7 | convolution fusion | flops 3651720192 | bytes 9821696 | tf_op jit(solution)/shard_map/bsd,bsf->df/dot_general | solution.py:203
  481.7 3.2 fusion.42
  485.0 6.4 convolution_convert_fusion.7
  491.4 13.2 %multiply_reduce_fusion = (f32[8,736]{1,0:T(8,128)S(1)}, f32[8,736,736]{1,2,0:T(8,128)}) fusion(f32[8,736,736]{1,2,0:T(8,128)} %get-tuple-element.122, f32[8,736]{1,0:T(8,128)S(1)} %log_add_fusion, pred[736]{0:T(1024)(128)(4,1)S(1)} %iota_compare_fusion, bf16[736,8,72]{0,2,1:T(8,128)(2,1)S(1)} %bitcast.108, bf16[736,8,72]{0,2,1:T(8,128)(2,1)S(1)} %bitcast.93), kind=kOutput, calls=%fused_computation.1 | convolution fusion | flops 645695744 | bytes 36412128 | tf_op jit(solution)/shard_map/while/body/eval_jaxpr/qhd,khd->hqk/dot_general | solution.py:84
  504.6 13.0 %multiply_convert_fusion = bf16[8,736,736]{1,2,0:T(8,128)(2,1)S(1)} fusion(f32[8,736,736]{1,2,0:T(8,128)} %get-tuple-element.124, f32[8,736,736]{1,2,0:T(8,128)} %get-tuple-element.122, f32[8,736]{1,0:T(8,128)S(1)} %get-tuple-element.123, f32[8,736]{1,0:T(8,128)S(1)} %log_add_fusion, pred[736]{0:T(1024)(128)(4,1)S(1)} %iota_compare_fusion), kind=kLoop, calls=%fused_computation | loop fusion | flops 26001408 | bytes 43383520 | tf_op jit(solution)/shard_map/while/body/eval_jaxpr/convert_element_type | solution.py:86
  517.7 2.8 multiply_convert_fusion.2
  523.1 5.5 fusion.11
  528.8 6.3 convolution_convert_fusion.2
  535.2 18.2 %copy.70 = bf16[1152,3,576]{2,1,0:T(4,128)(2,1)} copy(bf16[1152,3,576]{2,0,1:T(8,128)(2,1)S(1)} %convolution_convert_fusion.2) | data formatting | bytes 7962624
  553.4 12.4 %reshape.392 = bf16[1152,1728]{1,0:T(8,128)(2,1)} reshape(bf16[1152,3,576]{2,1,0:T(4,128)(2,1)} %copy.70) | data formatting | bytes 7962624
  565.9 2.1 pad_maximum_fusion.1
  568.3 62.1 %all-reduce.4 = (f32[2,576]{1,0:T(2,128)S(1)}, f32[2152]{0:T(1024)S(1)}) all-reduce(f32[2,576]{1,0:T(2,128)S(1)} %convert_reduce_fusion.1, f32[2152]{0:T(1024)S(1)} %get-tuple-element.125), channel_id=1, replica_groups=mesh['dp'=16,'tensor'=2] {'dp'}, use_global_device_ids=true, to_apply=%region_24.25 | all-reduce | flops 3304 | bytes 26432 | tf_op jit(solution)/shard_map/psum | solution.py:243
  634.5 1.8 fusion.50
  636.3 47.3 %reduce-scatter.27.cloned.1.call-done = bf16[72,2152]{1,0:T(8,128)(2,1)} async-done(((bf16[1152,2152]{1,0:T(8,128)(2,1)}), bf16[72,2152]{1,0:T(8,128)(2,1)}) %reduce-scatter.27.cloned.1.call-update) | async-done | bytes 309904
  685.4 26.8 %reduce-scatter.23.cloned.1.call-done = bf16[1,368,1152]{2,1,0:T(8,128)(2,1)} async-done(((bf16[1,736,1152]{2,1,0:T(8,128)(2,1)}), bf16[1,368,1152]{2,1,0:T(8,128)(2,1)}) %reduce-scatter.23.cloned.1.call-update) | async-done | bytes 847888 | tf_op jit(solution)/shard_map/reduce_scatter | solution.py:33
  712.1 1.8 convert_reduce_fusion.2
  713.9 2.0 fusion.28
  716.1 1.8 convert_reduce_fusion.5
  717.9 40.8 %all-reduce.3 = (f32[2,1152]{1,0:T(2,128)S(1)}, f32[4,1152]{1,0:T(4,128)S(1)}) all-reduce(f32[2,1152]{1,0:T(2,128)S(1)} %pad_maximum_fusion.6, f32[4,1152]{1,0:T(4,128)S(1)} %pad_maximum_fusion.4), channel_id=1, replica_groups=mesh['dp'=16,'tensor'=2] {'dp','tensor'}, use_global_device_ids=true, to_apply=%region_31.32 | all-reduce | flops 6912 | bytes 55296 | tf_op jit(solution)/shard_map/psum | solution.py:242
  761.3 27.2 %reduce-scatter.25.cloned.1.call-done = bf16[72,1728]{1,0:T(8,128)(2,1)} async-done(((bf16[1152,1728]{1,0:T(8,128)(2,1)}), bf16[72,1728]{1,0:T(8,128)(2,1)}) %reduce-scatter.25.cloned.1.call-update) | async-done | bytes 248848
  793.0 39.4 %psum.39 = f32[]{:T(128)} all-reduce(f32[]{:T(128)S(6)} %add.313), channel_id=1, replica_groups=mesh['dp'=16,'tensor'=2] {'dp','tensor'}, use_global_device_ids=true, to_apply=%region_39.40 | all-reduce | flops 1 | bytes 8 | tf_op jit(solution)/shard_map/psum | solution.py:249
  837.9 3.1 fusion.75
  (186 shorter events, 40.5 us)
Async XLA Ops:
  7.2 7.9 copy-start.19
  7.2 8.7 %copy-start.23 = (f32[576,72]{0,1:T(8,128)S(1)}, f32[576,72]{0,1:T(8,128)}, u32[]{:S(2)}) copy-start(f32[576,72]{0,1:T(8,128)} %param.33) | copy-start | bytes 497668
  7.2 39.3 %all-gather.9.cloned.1.call-start = ((), (), s32[]{:S(2)}) async-start(), calls=%async_computation.8 | async-start | bytes 2543616 | tf_op jit(solution)/shard_map/all_gather | solution.py:29
  8.7 8.6 %copy-start.40 = (f32[2,576]{1,0:T(2,128)S(1)}, f32[2,576]{1,0:T(2,128)}, u32[]{:S(2)}) copy-start(f32[2,576]{1,0:T(2,128)} %param.48) | copy-start | bytes 13828
  8.7 98.8 %copy-start.35 = (f32[368]{0:T(512)}, f32[368]{0:T(512)S(1)}, u32[]{:S(2)}) copy-start(f32[368]{0:T(512)S(1)} %broadcast_multiply_fusion.1) | copy-start | bytes 4420
  10.8 96.6 %copy-start.38 = (f32[368]{0:T(512)}, f32[368]{0:T(512)S(1)}, u32[]{:S(2)}) copy-start(f32[368]{0:T(512)S(1)} %fusion.61) | copy-start | bytes 4420
  11.6 95.8 %copy-start.30 = (f32[1152]{0:T(1024)}, f32[1152]{0:T(1024)S(1)}, u32[]{:S(2)}) copy-start(f32[1152]{0:T(1024)S(1)} %get-tuple-element.75) | copy-start | bytes 13828
  15.0 86.0 %all-gather.11.cloned.1.call-start = ((), (), s32[]{:S(2)}) async-start(), calls=%async_computation.9 | async-start | bytes 4700160 | tf_op jit(solution)/shard_map/all_gather | solution.py:181
  15.9 125.8 %all-gather.13.cloned.1.call-start = ((), (), s32[]{:S(2)}) async-start(), calls=%async_computation.10 | async-start | bytes 1566720 | tf_op jit(solution)/shard_map/all_gather | solution.py:185
  16.6 155.8 %reduce-scatter.17.cloned.1.call-start = ((), (), s32[]{:S(2)}) async-start(), calls=%async_computation.11 | async-start | bytes 2543616 | tf_op jit(solution)/shard_map/reduce_scatter | solution.py:33
  107.7 8.6 %copy-start.5 = (bf16[736,1,576]{0,2,1:T(8,128)(2,1)}, bf16[736,1,576]{0,2,1:T(8,128)(2,1)S(1)}, u32[]{:S(2)}) copy-start(bf16[736,1,576]{0,2,1:T(8,128)(2,1)S(1)} %get-tuple-element.113) | copy-start | bytes 2543620
  107.7 8.6 %copy-start.7 = (bf16[736,1,576]{0,2,1:T(8,128)(2,1)}, bf16[736,1,576]{0,2,1:T(8,128)(2,1)S(1)}, u32[]{:S(2)}) copy-start(bf16[736,1,576]{0,2,1:T(8,128)(2,1)S(1)} %get-tuple-element.114) | copy-start | bytes 2543620
  107.7 26.9 %copy-start.3 = (bf16[736,1,576]{0,2,1:T(8,128)(2,1)}, bf16[736,1,576]{0,2,1:T(8,128)(2,1)S(1)}, u32[]{:S(2)}) copy-start(bf16[736,1,576]{0,2,1:T(8,128)(2,1)S(1)} %get-tuple-element.115) | copy-start | bytes 2543620
  139.8 6.2 copy-start.20
  141.6 4.4 copy-start.17
  146.0 26.4 %copy-start = (bf16[1,368,1152]{2,1,0:T(8,128)(2,1)S(1)}, bf16[1,368,1152]{2,1,0:T(8,128)(2,1)}, u32[]{:S(2)}) copy-start(bf16[1,368,1152]{2,1,0:T(8,128)(2,1)} %param.27) | copy-start | bytes 2543620
  146.0 84.2 %all-gather.17.cloned.1.call-start = ((), (), s32[]{:S(2)}) async-start(), calls=%async_computation.13 | async-start | bytes 5326848 | tf_op jit(solution)/shard_map/all_gather | solution.py:182
  146.8 112.6 %all-gather.15.cloned.1.call-start = ((), (), s32[]{:S(2)}) async-start(), calls=%async_computation.12 | async-start | bytes 2543616 | tf_op jit(solution)/shard_map/all_gather | solution.py:29
  177.2 112.5 %all-gather.21.cloned.1.call-start = ((), (), s32[]{:S(2)}) async-start(), calls=%async_computation.16 | async-start | bytes 2543616 | tf_op jit(solution)/shard_map/all_gather | solution.py:29
  177.9 169.6 %all-gather.19.cloned.1.call-start = ((), (), s32[]{:S(2)}) async-start(), calls=%async_computation.14 | async-start | bytes 5326848 | tf_op jit(solution)/shard_map/all_gather | solution.py:186
  178.7 168.8 %copy-start.46 = (f32[2152]{0:T(1024)S(1)}, f32[2152]{0:T(1024)}, u32[]{:S(2)}) copy-start(f32[2152]{0:T(1024)} %param.51) | copy-start | bytes 25828
  178.8 216.0 %reduce-scatter.21.cloned.1.call-start = ((), (), s32[]{:S(2)}) async-start(), calls=%async_computation.17 | async-start | bytes 2543616 | tf_op jit(solution)/shard_map/reduce_scatter | solution.py:33
  368.7 55.7 %reduce-scatter.19.cloned.1.call-start = ((), (), s32[]{:S(2)}) async-start(), calls=%async_computation.15 | async-start | bytes 2543616 | tf_op jit(solution)/shard_map/reduce_scatter | solution.py:33
  380.0 77.7 %all-gather.23.cloned.1.call-start = ((), (), s32[]{:S(2)}) async-start(), calls=%async_computation.18 | async-start | bytes 2543616 | tf_op jit(solution)/shard_map/all_gather | solution.py:29
  428.9 204.0 %reduce-scatter.29.cloned.1.call-start = ((), (), s32[]{:S(2)}) async-start(), calls=%async_computation.22 | async-start | bytes 1566720
  462.2 172.3 %reduce-scatter.31.cloned.1.call-start = ((), (), s32[]{:S(2)}) async-start(), calls=%async_computation.23 | async-start | bytes 5326848
  472.5 211.1 %reduce-scatter.27.cloned.1.call-start = ((), (), s32[]{:S(2)}) async-start(), calls=%async_computation.21 | async-start | bytes 5326848
  481.7 230.4 %reduce-scatter.23.cloned.1.call-start = ((), (), s32[]{:S(2)}) async-start(), calls=%async_computation.19 | async-start | bytes 2543616 | tf_op jit(solution)/shard_map/reduce_scatter | solution.py:33
  485.0 6.4 copy-start.4
  491.4 30.7 %copy-start.13 = (bf16[8,72,736]{2,1,0:T(8,128)(2,1)}, bf16[8,72,736]{2,1,0:T(8,128)(2,1)S(1)}, u32[]{:S(2)}) copy-start(bf16[8,72,736]{2,1,0:T(8,128)(2,1)S(1)} %convolution_convert_fusion.7) | copy-start | bytes 2543620
  504.6 13.0 %copy-start.8 = (bf16[736,1,576]{0,2,1:T(8,128)(2,1)S(1)}, bf16[736,1,576]{0,2,1:T(8,128)(2,1)}, u32[]{:S(2)}) copy-start(bf16[736,1,576]{0,2,1:T(8,128)(2,1)} %copy-done.7) | copy-start | bytes 2543620
  517.7 5.4 slice-start
  528.6 259.9 %reduce-scatter.25.cloned.1.call-start = ((), (), s32[]{:S(2)}) async-start(), calls=%async_computation.20 | async-start | bytes 4386816
  565.8 146.3 %copy-start.31 = (f32[1152]{0:T(1024)S(1)}, f32[1152]{0:T(1024)}, u32[]{:S(2)}) copy-start(f32[1152]{0:T(1024)} %copy-done.30) | copy-start | bytes 13828
  565.9 146.3 %copy-start.36 = (f32[368]{0:T(512)S(1)}, f32[368]{0:T(512)}, u32[]{:S(2)}) copy-start(f32[368]{0:T(512)} %copy-done.35) | copy-start | bytes 4420
  567.9 146.0 %copy-start.45 = (f32[368]{0:T(512)S(1)}, f32[368]{0:T(512)}, u32[]{:S(2)}) copy-start(f32[368]{0:T(512)} %copy-done.44) | copy-start | bytes 4420
  568.0 146.0 %copy-start.39 = (f32[368]{0:T(512)S(1)}, f32[368]{0:T(512)}, u32[]{:S(2)}) copy-start(f32[368]{0:T(512)} %copy-done.38) | copy-start | bytes 4420
  568.0 148.0 %copy-start.10 = (bf16[1,368,1152]{2,1,0:T(8,128)(2,1)S(1)}, bf16[1,368,1152]{2,1,0:T(8,128)(2,1)}, u32[]{:S(2)}) copy-start(bf16[1,368,1152]{2,1,0:T(8,128)(2,1)} %param.28) | copy-start | bytes 2543620
  716.0 117.2 %copy-start.41 = (f32[2,576]{1,0:T(2,128)S(1)}, f32[2,576]{1,0:T(2,128)}, u32[]{:S(2)}) copy-start(f32[2,576]{1,0:T(2,128)} %param.48) | copy-start | bytes 13828
  716.0 118.5 %copy-start.37 = (f32[2,1152]{1,0:T(2,128)S(1)}, f32[2,1152]{1,0:T(2,128)}, u32[]{:S(2)}) copy-start(f32[2,1152]{1,0:T(2,128)} %param.42) | copy-start | bytes 27652
  716.0 121.2 %copy-start.34 = (f32[4,1152]{1,0:T(4,128)S(1)}, f32[4,1152]{1,0:T(4,128)}, u32[]{:S(2)}) copy-start(f32[4,1152]{1,0:T(4,128)} %param.45) | copy-start | bytes 55300
  716.1 121.2 %copy-start.42 = (f32[4,1152]{1,0:T(4,128)S(1)}, f32[4,1152]{1,0:T(4,128)}, u32[]{:S(2)}) copy-start(f32[4,1152]{1,0:T(4,128)} %param.46) | copy-start | bytes 55300
  716.1 121.2 %copy-start.43 = (f32[4,1152]{1,0:T(4,128)S(1)}, f32[4,1152]{1,0:T(4,128)}, u32[]{:S(2)}) copy-start(f32[4,1152]{1,0:T(4,128)} %param.47) | copy-start | bytes 55300
  759.4 81.7 %copy-start.24 = (f32[576,72]{0,1:T(8,128)S(1)}, f32[576,72]{0,1:T(8,128)}, u32[]{:S(2)}) copy-start(f32[576,72]{0,1:T(8,128)} %param.33) | copy-start | bytes 497668
  759.4 81.7 %copy-start.29 = (bf16[576,72]{0,1:T(8,128)(2,1)S(1)}, bf16[576,72]{0,1:T(8,128)(2,1)}, u32[]{:S(2)}) copy-start(bf16[576,72]{0,1:T(8,128)(2,1)} %reduce-scatter.29.cloned.1.call-done) | copy-start | bytes 248836
  759.4 81.7 %copy-start.32 = (f32[576,72]{0,1:T(8,128)S(1)}, f32[576,72]{0,1:T(8,128)}, u32[]{:S(2)}) copy-start(f32[576,72]{0,1:T(8,128)} %param.34) | copy-start | bytes 497668
  759.4 81.7 %copy-start.33 = (f32[576,72]{0,1:T(8,128)S(1)}, f32[576,72]{0,1:T(8,128)}, u32[]{:S(2)}) copy-start(f32[576,72]{0,1:T(8,128)} %param.35) | copy-start | bytes 497668
  837.9 4.1 copy-start.26
  (18 other events, 51.8 us)
Sparse Core Ops, SparseCore 0:
  15.2 31.2 all-gather.8
  49.3 51.7 all-gather.10
  103.8 37.8 all-gather.12
  146.1 26.2 reduce-scatter.16
  175.2 54.8 all-gather.16
  232.2 27.1 all-gather.14
  261.0 28.5 all-gather.20
  292.6 54.9 all-gather.18
  368.8 25.9 reduce-scatter.20
  396.9 27.4 reduce-scatter.18
  429.1 28.5 all-gather.22
  462.3 58.7 reduce-scatter.28
  525.6 77.2 reduce-scatter.30
  606.7 76.8 reduce-scatter.26
  685.8 26.2 reduce-scatter.22
  715.9 72.6 reduce-scatter.24
where the time goes:
time: 859 us; the launch traced here: 853 us
  waiting for transfers between devices  442 us (51%)
  blocking collectives  142 us (17%)
  matrix products  124 us (14%)
  other arithmetic  79.5 us (9%)
  local copies, waits for them, and re-layouts  40.6 us (5%)
  between operations  22.6 us (3%)
    all_gather x4, waiting for transfers between devices, whole_rows(): return lax.all_gather(part, 'tensor', axis=1, tiled=True)  107 us
    reduce_scatter x4, waiting for transfers between devices, share_rows(): lax.psum_scatter(full.astype(jnp.bfloat16), 'tensor', scatter_dimension=1...  94.5 us
    unnamed x20, waiting for transfers between devices  75.5 us
    psum x1, blocking collectives, on_device(): head_sum, hidden_sum = lax.psum((head_grad, hidden_grad), 'dp')  62.1 us
    all_gather x1, waiting for transfers between devices, on_device(): lax.all_gather(reduce_weight.astype(jnp.bfloat16), 'dp', axis=1, tiled=True)  57.9 us
    all_gather x1, waiting for transfers between devices, on_device(): lax.all_gather(joint_weight.astype(jnp.bfloat16), 'dp', axis=0, tiled=True)  54.5 us
    all_gather x1, waiting for transfers between devices, on_device(): lax.all_gather(expand_weight.astype(jnp.bfloat16), 'dp', axis=0, tiled=True)  50.8 us
    psum x1, blocking collectives, on_device(): gain_sum, shift_sum = lax.psum((gain_grad, shift_grad), ('dp', 'tensor'))  40.8 us
  transfers between devices with their start and end apart: 16, of which 14 were waited for; matrix products, arithmetic and copies ran while one was open for 22% of the time, Pallas kernels for 0%

commit v1 on v0

--- a/solution.py
+++ b/solution.py
@@ -246,7 +246,7 @@
     owned = squares(joint_sum) + squares(expand_sum) + squares(output_sum) + squares(reduce_sum)
     shared = (squares(head_sum) + squares(hidden_sum)) / data_count
     everywhere = (squares(gain_sum) + squares(shift_sum)) / (data_count * split_count)
-    grad_norm = jnp.sqrt(lax.psum(owned + shared + everywhere, ("dp", "tensor")))
+    grad_norm = jnp.sqrt(lax.psum(lax.psum(owned + shared + everywhere, "tensor"), "dp"))
     factor = clip_limit / jnp.maximum(grad_norm, clip_limit)
     joint_state = adamw_step(
         joint_weight, joint_sum, joint_moment, joint_square, factor, matrix_rate, decay_rate

time: 859 us -> 855 us (level)
    psum x1 -> x2, blocking collectives: 39.4 us -> 35.5 us  [the longest x1 30.1 us: on_device(): lax.psum(lax.psum(owned + shared + everywhere, 'tensor'), 'dp')]
where the time goes in v1:
time: 855 us; the launch traced here: 850 us
  waiting for transfers between devices  442 us (52%)
  blocking collectives  138 us (16%)
  matrix products  124 us (15%)
  other arithmetic  79.5 us (9%)
  local copies, waits for them, and re-layouts  40.6 us (5%)
  between operations  22.7 us (3%)
    all_gather x4, waiting for transfers between devices, whole_rows(): return lax.all_gather(part, 'tensor', axis=1, tiled=True)  107 us
    reduce_scatter x4, waiting for transfers between devices, share_rows(): lax.psum_scatter(full.astype(jnp.bfloat16), 'tensor', scatter_dimension=1...  94.5 us
    unnamed x20, waiting for transfers between devices  75.4 us
    psum x1, blocking collectives, on_device(): head_sum, hidden_sum = lax.psum((head_grad, hidden_grad), 'dp')  62.1 us
    all_gather x1, waiting for transfers between devices, on_device(): lax.all_gather(reduce_weight.astype(jnp.bfloat16), 'dp', axis=1, tiled=True)  57.9 us
    all_gather x1, waiting for transfers between devices, on_device(): lax.all_gather(joint_weight.astype(jnp.bfloat16), 'dp', axis=0, tiled=True)  54.5 us
    all_gather x1, waiting for transfers between devices, on_device(): lax.all_gather(expand_weight.astype(jnp.bfloat16), 'dp', axis=0, tiled=True)  50.8 us
    psum x1, blocking collectives, on_device(): gain_sum, shift_sum = lax.psum((gain_grad, shift_grad), ('dp', 'tensor'))  40.8 us
  transfers between devices with their start and end apart: 16, of which 14 were waited for; matrix products, arithmetic and copies ran while one was open for 22% of the time, Pallas kernels for 0%

profile of v1, /device:TPU:0, one launch (start us, length us, event | category | flops | bytes accessed | tf_op | source)
XLA Modules:
  0.0 849.6 jit_solution(4723418292910857077)
XLA Ops:
  12.6 2.4 fusion.23
  17.5 29.0 %all-gather.9.cloned.1.call-done = bf16[1,736,1152]{2,1,0:T(8,128)(2,1)} async-done(((bf16[1,368,1152]{2,1,0:T(8,128)(2,1)}), bf16[1,736,1152]{2,1,0:T(8,128)(2,1)}) %all-gather.9.cloned.1.call-update) | async-done | bytes 1695760 | tf_op jit(solution)/shard_map/all_gather | solution.py:29
  46.5 54.5 %all-gather.11.cloned.1.call-done = bf16[1152,3,576]{2,0,1:T(8,128)(2,1)} async-done(((bf16[72,3,576]{2,0,1:T(8,128)(2,1)}), bf16[1152,3,576]{2,0,1:T(8,128)(2,1)}) %all-gather.11.cloned.1.call-update) | async-done | bytes 3981328 | tf_op jit(solution)/shard_map/all_gather | solution.py:181
  101.0 6.4 add_convert_fusion
  107.7 8.6 %fusion = (f32[8,736]{1,0:T(8,128)S(1)}, f32[8,736,736]{1,2,0:T(8,128)}) fusion(pred[736]{0:T(1024)(128)(4,1)S(1)} %iota_compare_fusion, bf16[736,8,72]{0,2,1:T(8,128)(2,1)S(1)} %bitcast.96, bf16[736,8,72]{0,2,1:T(8,128)(2,1)S(1)} %bitcast.94), kind=kOutput, calls=%fused_computation.5 | convolution fusion | flops 637028608 | bytes 19054304 | tf_op jit(solution)/shard_map/while/body/eval_jaxpr/qhd,khd->hqk/dot_general | solution.py:55
  116.3 10.0 %exponential_reduce_fusion = f32[8,736]{1,0:T(8,128)S(1)} fusion(f32[8,736,736]{1,2,0:T(8,128)} %get-tuple-element.122, f32[8,736]{1,0:T(8,128)S(1)} %get-tuple-element.121, pred[736]{0:T(1024)(128)(4,1)S(1)} %iota_compare_fusion), kind=kLoop, calls=%fused_computation.3 | loop fusion | flops 17328384 | bytes 17382112 | tf_op jit(solution)/shard_map/while/body/eval_jaxpr/reduce_sum | solution.py:66
  126.3 8.2 fusion.1
  134.6 3.5 copy-done.1
  139.8 1.8 all-gather.13.cloned.1.call-done
  141.6 4.3 fusion.10
  146.9 25.5 %reduce-scatter.17.cloned.1.call-done = bf16[1,368,1152]{2,1,0:T(8,128)(2,1)} async-done(((bf16[1,736,1152]{2,1,0:T(8,128)(2,1)}), bf16[1,368,1152]{2,1,0:T(8,128)(2,1)}) %reduce-scatter.17.cloned.1.call-update) | async-done | bytes 847888 | tf_op jit(solution)/shard_map/reduce_scatter | solution.py:33
  179.3 50.8 %all-gather.17.cloned.1.call-done = bf16[1152,2152]{1,0:T(8,128)(2,1)} async-done(((bf16[72,2152]{1,0:T(8,128)(2,1)}), bf16[1152,2152]{1,0:T(8,128)(2,1)}) %all-gather.17.cloned.1.call-update) | async-done | bytes 4958224 | tf_op jit(solution)/shard_map/all_gather | solution.py:182
  230.1 29.2 %all-gather.15.cloned.1.call-done = bf16[1,736,1152]{2,1,0:T(8,128)(2,1)} async-done(((bf16[1,368,1152]{2,1,0:T(8,128)(2,1)}), bf16[1,736,1152]{2,1,0:T(8,128)(2,1)}) %all-gather.15.cloned.1.call-update) | async-done | bytes 1695760 | tf_op jit(solution)/shard_map/all_gather | solution.py:29
  259.4 10.1 %fusion.38 = f32[736,2152]{1,0:T(8,128)} fusion(bf16[1152,2152]{1,0:T(8,128)(2,1)} %all-gather.17.cloned.1.call-done, bf16[1,736,1152]{2,1,0:T(8,128)(2,1)} %all-gather.15.cloned.1.call-done), kind=kOutput, calls=%fused_computation.72 | convolution fusion | flops 3649241088 | bytes 12989440 | tf_op jit(solution)/shard_map/bsd,df->bsf/dot_general | solution.py:115
  269.5 20.1 %all-gather.21.cloned.1.call-done = bf16[1,736,1152]{2,1,0:T(8,128)(2,1)} async-done(((bf16[1,368,1152]{2,1,0:T(8,128)(2,1)}), bf16[1,736,1152]{2,1,0:T(8,128)(2,1)}) %all-gather.21.cloned.1.call-update) | async-done | bytes 1695760 | tf_op jit(solution)/shard_map/all_gather | solution.py:29
  289.6 57.9 %all-gather.19.cloned.1.call-done = bf16[2152,1152]{0,1:T(8,128)(2,1)} async-done(((bf16[2152,72]{0,1:T(8,128)(2,1)}), bf16[2152,1152]{0,1:T(8,128)(2,1)}) %all-gather.19.cloned.1.call-update) | async-done | bytes 4958224 | tf_op jit(solution)/shard_map/all_gather | solution.py:186
  347.5 11.3 %convert_reduce_fusion = (f32[2152]{0:T(1024)S(1)}, bf16[736,2152]{1,0:T(8,128)(2,1)S(1)}) fusion(f32[736,2152]{1,0:T(8,128)} %fusion.38, f32[2152]{0:T(1024)S(1)} %copy-done.46, bf16[2152,1152]{0,1:T(8,128)(2,1)} %all-gather.19.cloned.1.call-done, bf16[1,736,1152]{2,1,0:T(8,128)(2,1)} %all-gather.21.cloned.1.call-done), kind=kOutput, calls=%fused_computation.18 | convolution fusion | flops 3685668096 | bytes 16174400 | tf_op jit(solution)/shard_map/bsd,fd->bsf/dot_general | solution.py:199
  360.5 8.2 fusion.13
  368.9 11.1 %fusion.12 = bf16[1,736,1152]{2,1,0:T(8,128)(2,1)} fusion(bf16[2152,1152]{0,1:T(8,128)(2,1)} %all-gather.19.cloned.1.call-done, f32[736,2152]{1,0:T(8,128)} %fusion.38, f32[2152]{0:T(1024)S(1)} %copy-done.46), kind=kOutput, calls=%fused_computation.31 | convolution fusion | flops 3665927680 | bytes 12998048 | tf_op jit(solution)/shard_map/bsf,fd->bsd/dot_general | solution.py:121
  380.1 14.7 %reduce-scatter.21.cloned.1.call-done = bf16[1,368,1152]{2,1,0:T(8,128)(2,1)} async-done(((bf16[1,736,1152]{2,1,0:T(8,128)(2,1)}), bf16[1,368,1152]{2,1,0:T(8,128)(2,1)}) %reduce-scatter.21.cloned.1.call-update) | async-done | bytes 847888 | tf_op jit(solution)/shard_map/reduce_scatter | solution.py:33
  394.8 2.0 fusion.27
  396.8 27.5 %reduce-scatter.19.cloned.1.call-done = bf16[1,368,1152]{2,1,0:T(8,128)(2,1)} async-done(((bf16[1,736,1152]{2,1,0:T(8,128)(2,1)}), bf16[1,368,1152]{2,1,0:T(8,128)(2,1)}) %reduce-scatter.19.cloned.1.call-update) | async-done | bytes 847888 | tf_op jit(solution)/shard_map/reduce_scatter | solution.py:33
  424.4 3.3 fusion.78
  429.0 28.7 %all-gather.23.cloned.1.call-done = bf16[1,736,1152]{2,1,0:T(8,128)(2,1)} async-done(((bf16[1,368,1152]{2,1,0:T(8,128)(2,1)}), bf16[1,736,1152]{2,1,0:T(8,128)(2,1)}) %all-gather.23.cloned.1.call-update) | async-done | bytes 1695760 | tf_op jit(solution)/shard_map/all_gather | solution.py:29
  457.7 4.5 convolution_convert_fusion.6
  462.4 10.1 %convolution_convert_fusion = bf16[2152,1152]{0,1:T(8,128)(2,1)} fusion(bf16[1,736,1152]{2,1,0:T(8,128)(2,1)} %all-gather.21.cloned.1.call-done, f32[736,2152]{1,0:T(8,128)} %fusion.38, f32[2152]{0:T(1024)S(1)} %copy-done.46), kind=kOutput, calls=%fused_computation.6 | convolution fusion | flops 3667558912 | bytes 12998048 | tf_op jit(solution)/shard_map/bsf,bsd->fd/dot_general | solution.py:198
  472.6 9.1 %convolution_convert_fusion.1 = bf16[1152,2152]{1,0:T(8,128)(2,1)} fusion(bf16[736,2152]{1,0:T(8,128)(2,1)} %copy-done.47, bf16[1,736,1152]{2,1,0:T(8,128)(2,1)} %all-gather.15.cloned.1.call-done), kind=kOutput, calls=%fused_computation.7 | convolution fusion | flops 3651720192 | bytes 9821696 | tf_op jit(solution)/shard_map/bsd,bsf->df/dot_general | solution.py:203
  481.7 3.2 fusion.42
  485.0 6.4 convolution_convert_fusion.7
  491.4 13.2 %multiply_reduce_fusion = (f32[8,736]{1,0:T(8,128)S(1)}, f32[8,736,736]{1,2,0:T(8,128)}) fusion(f32[8,736,736]{1,2,0:T(8,128)} %get-tuple-element.122, f32[8,736]{1,0:T(8,128)S(1)} %log_add_fusion, pred[736]{0:T(1024)(128)(4,1)S(1)} %iota_compare_fusion, bf16[736,8,72]{0,2,1:T(8,128)(2,1)S(1)} %bitcast.108, bf16[736,8,72]{0,2,1:T(8,128)(2,1)S(1)} %bitcast.93), kind=kOutput, calls=%fused_computation.1 | convolution fusion | flops 645695744 | bytes 36412128 | tf_op jit(solution)/shard_map/while/body/eval_jaxpr/qhd,khd->hqk/dot_general | solution.py:84
  504.6 13.0 %multiply_convert_fusion = bf16[8,736,736]{1,2,0:T(8,128)(2,1)S(1)} fusion(f32[8,736,736]{1,2,0:T(8,128)} %get-tuple-element.124, f32[8,736,736]{1,2,0:T(8,128)} %get-tuple-element.122, f32[8,736]{1,0:T(8,128)S(1)} %get-tuple-element.123, f32[8,736]{1,0:T(8,128)S(1)} %log_add_fusion, pred[736]{0:T(1024)(128)(4,1)S(1)} %iota_compare_fusion), kind=kLoop, calls=%fused_computation | loop fusion | flops 26001408 | bytes 43383520 | tf_op jit(solution)/shard_map/while/body/eval_jaxpr/convert_element_type | solution.py:86
  517.7 2.8 multiply_convert_fusion.2
  523.1 5.5 fusion.11
  528.8 6.3 convolution_convert_fusion.2
  535.2 18.2 %copy.70 = bf16[1152,3,576]{2,1,0:T(4,128)(2,1)} copy(bf16[1152,3,576]{2,0,1:T(8,128)(2,1)S(1)} %convolution_convert_fusion.2) | data formatting | bytes 7962624
  553.4 12.4 %reshape.392 = bf16[1152,1728]{1,0:T(8,128)(2,1)} reshape(bf16[1152,3,576]{2,1,0:T(4,128)(2,1)} %copy.70) | data formatting | bytes 7962624
  565.9 2.1 pad_maximum_fusion.1
  568.3 62.1 %all-reduce.4 = (f32[2,576]{1,0:T(2,128)S(1)}, f32[2152]{0:T(1024)S(1)}) all-reduce(f32[2,576]{1,0:T(2,128)S(1)} %convert_reduce_fusion.1, f32[2152]{0:T(1024)S(1)} %get-tuple-element.125), channel_id=1, replica_groups=mesh['dp'=16,'tensor'=2] {'dp'}, use_global_device_ids=true, to_apply=%region_24.25 | all-reduce | flops 3304 | bytes 26432 | tf_op jit(solution)/shard_map/psum | solution.py:243
  634.5 1.8 fusion.50
  636.3 47.3 %reduce-scatter.27.cloned.1.call-done = bf16[72,2152]{1,0:T(8,128)(2,1)} async-done(((bf16[1152,2152]{1,0:T(8,128)(2,1)}), bf16[72,2152]{1,0:T(8,128)(2,1)}) %reduce-scatter.27.cloned.1.call-update) | async-done | bytes 309904
  685.4 26.8 %reduce-scatter.23.cloned.1.call-done = bf16[1,368,1152]{2,1,0:T(8,128)(2,1)} async-done(((bf16[1,736,1152]{2,1,0:T(8,128)(2,1)}), bf16[1,368,1152]{2,1,0:T(8,128)(2,1)}) %reduce-scatter.23.cloned.1.call-update) | async-done | bytes 847888 | tf_op jit(solution)/shard_map/reduce_scatter | solution.py:33
  713.9 2.0 fusion.28
  716.1 1.8 convert_reduce_fusion.5
  717.9 40.8 %all-reduce.3 = (f32[2,1152]{1,0:T(2,128)S(1)}, f32[4,1152]{1,0:T(4,128)S(1)}) all-reduce(f32[2,1152]{1,0:T(2,128)S(1)} %pad_maximum_fusion.6, f32[4,1152]{1,0:T(4,128)S(1)} %pad_maximum_fusion.4), channel_id=1, replica_groups=mesh['dp'=16,'tensor'=2] {'dp','tensor'}, use_global_device_ids=true, to_apply=%region_31.32 | all-reduce | flops 6912 | bytes 55296 | tf_op jit(solution)/shard_map/psum | solution.py:242
  761.4 27.2 %reduce-scatter.25.cloned.1.call-done = bf16[72,1728]{1,0:T(8,128)(2,1)} async-done(((bf16[1152,1728]{1,0:T(8,128)(2,1)}), bf16[72,1728]{1,0:T(8,128)(2,1)}) %reduce-scatter.25.cloned.1.call-update) | async-done | bytes 248848
  793.0 5.4 psum.46
  798.5 30.1 %psum.47 = f32[]{:T(128)} all-reduce(f32[]{:T(128)} %psum.46), channel_id=1, replica_groups=mesh['dp'=16,'tensor'=2] {'dp'}, use_global_device_ids=true, to_apply=%region_40.41 | all-reduce | flops 1 | bytes 8 | tf_op jit(solution)/shard_map/psum | solution.py:249
  834.0 3.1 fusion.75
  (187 shorter events, 42.3 us)
Async XLA Ops:
  7.2 7.9 copy-start.19
  7.2 8.7 %copy-start.23 = (f32[576,72]{0,1:T(8,128)S(1)}, f32[576,72]{0,1:T(8,128)}, u32[]{:S(2)}) copy-start(f32[576,72]{0,1:T(8,128)} %param.33) | copy-start | bytes 497668
  7.2 39.3 %all-gather.9.cloned.1.call-start = ((), (), s32[]{:S(2)}) async-start(), calls=%async_computation.8 | async-start | bytes 2543616 | tf_op jit(solution)/shard_map/all_gather | solution.py:29
  8.7 8.6 %copy-start.40 = (f32[2,576]{1,0:T(2,128)S(1)}, f32[2,576]{1,0:T(2,128)}, u32[]{:S(2)}) copy-start(f32[2,576]{1,0:T(2,128)} %param.48) | copy-start | bytes 13828
  8.7 98.8 %copy-start.35 = (f32[368]{0:T(512)}, f32[368]{0:T(512)S(1)}, u32[]{:S(2)}) copy-start(f32[368]{0:T(512)S(1)} %broadcast_multiply_fusion.1) | copy-start | bytes 4420
  10.8 96.6 %copy-start.38 = (f32[368]{0:T(512)}, f32[368]{0:T(512)S(1)}, u32[]{:S(2)}) copy-start(f32[368]{0:T(512)S(1)} %fusion.61) | copy-start | bytes 4420
  11.6 95.8 %copy-start.30 = (f32[1152]{0:T(1024)}, f32[1152]{0:T(1024)S(1)}, u32[]{:S(2)}) copy-start(f32[1152]{0:T(1024)S(1)} %get-tuple-element.75) | copy-start | bytes 13828
  15.0 86.0 %all-gather.11.cloned.1.call-start = ((), (), s32[]{:S(2)}) async-start(), calls=%async_computation.9 | async-start | bytes 4700160 | tf_op jit(solution)/shard_map/all_gather | solution.py:181
  15.9 125.8 %all-gather.13.cloned.1.call-start = ((), (), s32[]{:S(2)}) async-start(), calls=%async_computation.10 | async-start | bytes 1566720 | tf_op jit(solution)/shard_map/all_gather | solution.py:185
  16.6 155.8 %reduce-scatter.17.cloned.1.call-start = ((), (), s32[]{:S(2)}) async-start(), calls=%async_computation.11 | async-start | bytes 2543616 | tf_op jit(solution)/shard_map/reduce_scatter | solution.py:33
  107.7 8.6 %copy-start.5 = (bf16[736,1,576]{0,2,1:T(8,128)(2,1)}, bf16[736,1,576]{0,2,1:T(8,128)(2,1)S(1)}, u32[]{:S(2)}) copy-start(bf16[736,1,576]{0,2,1:T(8,128)(2,1)S(1)} %get-tuple-element.113) | copy-start | bytes 2543620
  107.7 8.6 %copy-start.7 = (bf16[736,1,576]{0,2,1:T(8,128)(2,1)}, bf16[736,1,576]{0,2,1:T(8,128)(2,1)S(1)}, u32[]{:S(2)}) copy-start(bf16[736,1,576]{0,2,1:T(8,128)(2,1)S(1)} %get-tuple-element.114) | copy-start | bytes 2543620
  107.7 26.9 %copy-start.3 = (bf16[736,1,576]{0,2,1:T(8,128)(2,1)}, bf16[736,1,576]{0,2,1:T(8,128)(2,1)S(1)}, u32[]{:S(2)}) copy-start(bf16[736,1,576]{0,2,1:T(8,128)(2,1)S(1)} %get-tuple-element.115) | copy-start | bytes 2543620
  139.8 6.2 copy-start.20
  141.6 4.4 copy-start.17
  146.0 26.4 %copy-start = (bf16[1,368,1152]{2,1,0:T(8,128)(2,1)S(1)}, bf16[1,368,1152]{2,1,0:T(8,128)(2,1)}, u32[]{:S(2)}) copy-start(bf16[1,368,1152]{2,1,0:T(8,128)(2,1)} %param.27) | copy-start | bytes 2543620
  146.0 84.2 %all-gather.17.cloned.1.call-start = ((), (), s32[]{:S(2)}) async-start(), calls=%async_computation.13 | async-start | bytes 5326848 | tf_op jit(solution)/shard_map/all_gather | solution.py:182
  146.8 112.6 %all-gather.15.cloned.1.call-start = ((), (), s32[]{:S(2)}) async-start(), calls=%async_computation.12 | async-start | bytes 2543616 | tf_op jit(solution)/shard_map/all_gather | solution.py:29
  177.2 112.5 %all-gather.21.cloned.1.call-start = ((), (), s32[]{:S(2)}) async-start(), calls=%async_computation.16 | async-start | bytes 2543616 | tf_op jit(solution)/shard_map/all_gather | solution.py:29
  177.9 169.6 %all-gather.19.cloned.1.call-start = ((), (), s32[]{:S(2)}) async-start(), calls=%async_computation.14 | async-start | bytes 5326848 | tf_op jit(solution)/shard_map/all_gather | solution.py:186
  178.7 168.8 %copy-start.46 = (f32[2152]{0:T(1024)S(1)}, f32[2152]{0:T(1024)}, u32[]{:S(2)}) copy-start(f32[2152]{0:T(1024)} %param.51) | copy-start | bytes 25828
  178.8 216.0 %reduce-scatter.21.cloned.1.call-start = ((), (), s32[]{:S(2)}) async-start(), calls=%async_computation.17 | async-start | bytes 2543616 | tf_op jit(solution)/shard_map/reduce_scatter | solution.py:33
  368.7 55.7 %reduce-scatter.19.cloned.1.call-start = ((), (), s32[]{:S(2)}) async-start(), calls=%async_computation.15 | async-start | bytes 2543616 | tf_op jit(solution)/shard_map/reduce_scatter | solution.py:33
  380.0 77.7 %all-gather.23.cloned.1.call-start = ((), (), s32[]{:S(2)}) async-start(), calls=%async_computation.18 | async-start | bytes 2543616 | tf_op jit(solution)/shard_map/all_gather | solution.py:29
  428.9 204.0 %reduce-scatter.29.cloned.1.call-start = ((), (), s32[]{:S(2)}) async-start(), calls=%async_computation.22 | async-start | bytes 1566720
  462.2 172.3 %reduce-scatter.31.cloned.1.call-start = ((), (), s32[]{:S(2)}) async-start(), calls=%async_computation.23 | async-start | bytes 5326848
  472.5 211.1 %reduce-scatter.27.cloned.1.call-start = ((), (), s32[]{:S(2)}) async-start(), calls=%async_computation.21 | async-start | bytes 5326848
  481.7 230.4 %reduce-scatter.23.cloned.1.call-start = ((), (), s32[]{:S(2)}) async-start(), calls=%async_computation.19 | async-start | bytes 2543616 | tf_op jit(solution)/shard_map/reduce_scatter | solution.py:33
  485.0 6.4 copy-start.4
  491.4 30.7 %copy-start.13 = (bf16[8,72,736]{2,1,0:T(8,128)(2,1)}, bf16[8,72,736]{2,1,0:T(8,128)(2,1)S(1)}, u32[]{:S(2)}) copy-start(bf16[8,72,736]{2,1,0:T(8,128)(2,1)S(1)} %convolution_convert_fusion.7) | copy-start | bytes 2543620
  504.6 13.0 %copy-start.8 = (bf16[736,1,576]{0,2,1:T(8,128)(2,1)S(1)}, bf16[736,1,576]{0,2,1:T(8,128)(2,1)}, u32[]{:S(2)}) copy-start(bf16[736,1,576]{0,2,1:T(8,128)(2,1)} %copy-done.7) | copy-start | bytes 2543620
  517.7 5.4 slice-start
  528.6 259.9 %reduce-scatter.25.cloned.1.call-start = ((), (), s32[]{:S(2)}) async-start(), calls=%async_computation.20 | async-start | bytes 4386816
  565.8 146.3 %copy-start.31 = (f32[1152]{0:T(1024)S(1)}, f32[1152]{0:T(1024)}, u32[]{:S(2)}) copy-start(f32[1152]{0:T(1024)} %copy-done.30) | copy-start | bytes 13828
  565.9 146.3 %copy-start.36 = (f32[368]{0:T(512)S(1)}, f32[368]{0:T(512)}, u32[]{:S(2)}) copy-start(f32[368]{0:T(512)} %copy-done.35) | copy-start | bytes 4420
  567.9 146.0 %copy-start.45 = (f32[368]{0:T(512)S(1)}, f32[368]{0:T(512)}, u32[]{:S(2)}) copy-start(f32[368]{0:T(512)} %copy-done.44) | copy-start | bytes 4420
  568.0 146.0 %copy-start.39 = (f32[368]{0:T(512)S(1)}, f32[368]{0:T(512)}, u32[]{:S(2)}) copy-start(f32[368]{0:T(512)} %copy-done.38) | copy-start | bytes 4420
  568.0 148.0 %copy-start.10 = (bf16[1,368,1152]{2,1,0:T(8,128)(2,1)S(1)}, bf16[1,368,1152]{2,1,0:T(8,128)(2,1)}, u32[]{:S(2)}) copy-start(bf16[1,368,1152]{2,1,0:T(8,128)(2,1)} %param.28) | copy-start | bytes 2543620
  716.0 113.3 %copy-start.41 = (f32[2,576]{1,0:T(2,128)S(1)}, f32[2,576]{1,0:T(2,128)}, u32[]{:S(2)}) copy-start(f32[2,576]{1,0:T(2,128)} %param.48) | copy-start | bytes 13828
  716.0 114.6 %copy-start.37 = (f32[2,1152]{1,0:T(2,128)S(1)}, f32[2,1152]{1,0:T(2,128)}, u32[]{:S(2)}) copy-start(f32[2,1152]{1,0:T(2,128)} %param.42) | copy-start | bytes 27652
  716.0 117.3 %copy-start.34 = (f32[4,1152]{1,0:T(4,128)S(1)}, f32[4,1152]{1,0:T(4,128)}, u32[]{:S(2)}) copy-start(f32[4,1152]{1,0:T(4,128)} %param.45) | copy-start | bytes 55300
  716.1 117.3 %copy-start.42 = (f32[4,1152]{1,0:T(4,128)S(1)}, f32[4,1152]{1,0:T(4,128)}, u32[]{:S(2)}) copy-start(f32[4,1152]{1,0:T(4,128)} %param.46) | copy-start | bytes 55300
  716.1 117.3 %copy-start.43 = (f32[4,1152]{1,0:T(4,128)S(1)}, f32[4,1152]{1,0:T(4,128)}, u32[]{:S(2)}) copy-start(f32[4,1152]{1,0:T(4,128)} %param.47) | copy-start | bytes 55300
  760.0 77.2 %copy-start.24 = (f32[576,72]{0,1:T(8,128)S(1)}, f32[576,72]{0,1:T(8,128)}, u32[]{:S(2)}) copy-start(f32[576,72]{0,1:T(8,128)} %param.33) | copy-start | bytes 497668
  760.0 77.2 %copy-start.29 = (bf16[576,72]{0,1:T(8,128)(2,1)S(1)}, bf16[576,72]{0,1:T(8,128)(2,1)}, u32[]{:S(2)}) copy-start(bf16[576,72]{0,1:T(8,128)(2,1)} %reduce-scatter.29.cloned.1.call-done) | copy-start | bytes 248836
  760.0 77.2 %copy-start.32 = (f32[576,72]{0,1:T(8,128)S(1)}, f32[576,72]{0,1:T(8,128)}, u32[]{:S(2)}) copy-start(f32[576,72]{0,1:T(8,128)} %param.34) | copy-start | bytes 497668
  760.0 77.2 %copy-start.33 = (f32[576,72]{0,1:T(8,128)S(1)}, f32[576,72]{0,1:T(8,128)}, u32[]{:S(2)}) copy-start(f32[576,72]{0,1:T(8,128)} %param.35) | copy-start | bytes 497668
  834.0 4.1 copy-start.26
  (18 other events, 51.8 us)
Sparse Core Ops, SparseCore 0:
  15.2 31.2 all-gather.8
  49.3 51.7 all-gather.10
  103.8 37.8 all-gather.12
  146.1 26.2 reduce-scatter.16
  175.2 54.8 all-gather.16
  232.2 27.1 all-gather.14
  261.0 28.5 all-gather.20
  292.6 54.9 all-gather.18
  368.8 25.9 reduce-scatter.20
  396.9 27.4 reduce-scatter.18
  429.1 28.5 all-gather.22
  462.3 58.7 reduce-scatter.28
  525.6 77.2 reduce-scatter.30
  606.7 76.8 reduce-scatter.26
  685.8 26.2 reduce-scatter.22
  715.9 72.6 reduce-scatter.24
